TPU v7x, 128 devices: a whole 4x4x4 slice. The times are simulated.
128 devices in a mesh: tiles: 16 (over y, z), rows: 8 (over x, core).
Axes of the slice: x: 4, y: 4, z: 4, core: 2. Of those that a mesh axis runs over, the one named last changes fastest.
Arguments:
- tile_values: bfloat16 [512, 128, 128, 128], P(('tiles', 'rows')), may hold values from -6 to 6
- tile_coords: int32 [256, 3], replicated, may hold values from 0 to 127, as said below
- tile_owner: int32 [256], replicated, may hold values from 0 to 127, as said below
- factor_b: bfloat16 [16384, 128], P('rows')
- factor_c: bfloat16 [16384, 128], P('rows')
Outputs:
- factor_a: float32 [16384, 128], P('rows')
Inputs may be any that keep to these rules, and one draw needn't show every extreme that they name: `tile_owner`: devices are numbered along tiles then rows. A device holds at most 4 tiles, and in every draw some device holds exactly 4; its tiles fill its first slots in increasing order of tile number. `tile_coords`: no two tiles have the same block indices.
All inputs are finite; a program needn't handle non-finite values.
Results may differ from a plain program's by a relative error of at most 0.0003.
Values may be sent and summed in bfloat16 or wider, within the bound.
No kernel may reach another device: no remote copies, remote signals or barrier semaphores. Data moves between devices by JAX's collectives and lax.ppermute only.
A program may use at most 128 MiB of HBM per device.

v0:
```python
import jax
import jax.numpy as jnp
from jax import lax
from jax.sharding import PartitionSpec as P


def slot_table(device, tile_coords, tile_owner, slot_count):
    mine = (tile_owner == device).astype(jnp.int32)
    order = jnp.cumsum(mine) - 1
    matches = (mine[None, :] == 1) & (
        order[None, :] == jnp.arange(slot_count, dtype=jnp.int32)[:, None]
    )
    present = jnp.any(matches, axis=1)
    placed = jnp.sum(matches.astype(jnp.int32)[:, :, None] * tile_coords[None, :, :], axis=1)
    return (placed, present)


def factor_gram(block_rows):
    return lax.dot_general(
        block_rows, block_rows, (((0,), (0,)), ((), ())), preferred_element_type=jnp.float32
    )


def body(tile_values, tile_coords, tile_owner, factor_b, factor_c):
    slot_count = tile_values.shape[0]
    tile_edge = tile_values.shape[1]
    rank_width = factor_b.shape[1]
    tiles_count = lax.axis_size("tiles")
    rows_count = lax.axis_size("rows")
    tiles_index = lax.axis_index("tiles")
    rows_index = lax.axis_index("rows")
    shard_rows = factor_b.shape[0]
    owned_rows = shard_rows // tiles_count
    blocks_unit = owned_rows // tile_edge
    edge_range = jnp.arange(tile_edge, dtype=jnp.int32)
    device = tiles_index * rows_count + rows_index
    coords, present = slot_table(device, tile_coords, tile_owner, slot_count)
    need_b = (coords[:, 1][:, None] * tile_edge + edge_range[None, :]).reshape(-1)
    need_c = (coords[:, 2][:, None] * tile_edge + edge_range[None, :]).reshape(-1)
    blank = jnp.zeros((slot_count * tile_edge, rank_width), jnp.bfloat16)
    carry = (blank, blank)
    pieces = (
        lax.all_gather(factor_b, "rows", axis=0, tiled=True),
        lax.all_gather(factor_c, "rows", axis=0, tiled=True),
    )
    results = []
    for held, piece, needed in zip(carry, pieces, (need_b, need_c)):
        inside = (needed >= 0) & (needed < piece.shape[0])
        taken = jnp.take(piece, jnp.clip(needed, 0, piece.shape[0] - 1), axis=0)
        results.append(jnp.where(inside[:, None], taken, held))
    chosen_b = results[0]
    chosen_c = results[1]

    def contract(position, partials):
        tile = lax.dynamic_index_in_dim(tile_values, position, 0, keepdims=False).reshape(
            tile_edge * tile_edge, tile_edge
        )
        block_c = lax.dynamic_slice_in_dim(chosen_c, position * tile_edge, tile_edge, 0)
        block_b = lax.dynamic_slice_in_dim(chosen_b, position * tile_edge, tile_edge, 0)
        inner = jnp.dot(tile, block_c, preferred_element_type=jnp.float32).reshape(
            tile_edge, tile_edge, rank_width
        )
        contrib = jnp.sum(inner * block_b.astype(jnp.float32)[None, :, :], axis=1)
        return lax.dynamic_update_index_in_dim(partials, contrib, position, 0)

    live_count = jnp.sum(present.astype(jnp.int32))
    partials = lax.fori_loop(
        0, live_count, contract, jnp.zeros((slot_count, tile_edge, rank_width), jnp.float32)
    )
    first_blocks = coords[:, 0]
    block_rows = jnp.arange(
        lax.axis_size(("tiles", "rows")) * owned_rows // tile_edge, dtype=jnp.int32
    )
    unit_index = block_rows // blocks_unit
    offset = block_rows % blocks_unit
    global_block = (
        unit_index % rows_count * tiles_count + unit_index // rows_count
    ) * blocks_unit + offset
    one_hot = ((global_block[:, None] == first_blocks[None, :]) & present[None, :]).astype(
        jnp.float32
    )
    summed = jnp.einsum("qs,sur->qur", one_hot, partials, precision=lax.Precision.HIGHEST)
    owned_sums = lax.psum_scatter(
        summed.reshape(lax.axis_size(("tiles", "rows")) * owned_rows, rank_width),
        ("tiles", "rows"),
        scatter_dimension=0,
        tiled=True,
    )
    gram_b, gram_c = lax.psum((factor_gram(factor_b), factor_gram(factor_c)), "rows")
    normal = gram_b * gram_c
    lower = jnp.linalg.cholesky(normal)
    solved = jax.scipy.linalg.cho_solve((lower, True), owned_sums.T).T
    return lax.all_gather(solved, "tiles", axis=0, tiled=True)


def solution(mesh):
    in_specs = (P(("tiles", "rows"), None, None, None), P(), P(), P("rows", None), P("rows", None))
    out_specs = P("rows", None)
    return jax.shard_map(body, mesh=mesh, in_specs=in_specs, out_specs=out_specs, check_vma=False)
```

profile of v0, /device:TPU:0, one launch (start us, length us, event | category | flops | bytes accessed | tf_op | source)
XLA Modules:
  0.0 838.5 jit_solution(6141258442397975768)
XLA Ops:
  6.5 0.0 all-gather.6.cloned.1.call-start
  6.5 0.7 all-gather.6.cloned.1.call-update
  7.3 0.0 all-gather.4.cloned.1.call-start
  7.3 0.7 all-gather.4.cloned.1.call-update
  8.0 0.0 all-reduce.3.cloned.1.call-start
  8.1 2.2 fusion.36
  10.2 2.2 fusion.37
  12.4 0.0 all-reduce.3.cloned.1.call-update
  12.4 0.0 reduce-scatter.2.cloned.1.call-start
  12.5 0.7 fusion.33
  13.2 0.3 reduce-window.9
  13.5 0.1 slice.34
  13.6 0.1 slice_reduce_fusion
  13.7 0.1 add_bitcast_fusion
  13.8 0.1 fusion.16
  13.9 0.8 multiply_reduce_fusion.1
  14.7 0.1 fusion.22
  14.8 0.1 compare_and_fusion
  14.9 0.1 compare_select_fusion
  15.0 0.1 compare_select_fusion.1
  15.1 0.6 convert_reduce_fusion
  15.7 27.9 %all-gather.6.cloned.1.call-done = bf16[16384,128]{1,0:T(8,128)(2,1)} async-done(((bf16[2048,128]{1,0:T(8,128)(2,1)}), bf16[16384,128]{1,0:T(8,128)(2,1)}) %all-gather.6.cloned.1.call-update) | async-done | bytes 4194320 | tf_op jit(solution)/shard_map/all_gather | solution.py:43
  43.6 3.8 gather_fusion.1
  47.4 0.2 select_select_fusion
  47.6 29.8 %all-gather.4.cloned.1.call-done = bf16[16384,128]{1,0:T(8,128)(2,1)} async-done(((bf16[2048,128]{1,0:T(8,128)(2,1)}), bf16[16384,128]{1,0:T(8,128)(2,1)}) %all-gather.4.cloned.1.call-update) | async-done | bytes 4194320 | tf_op jit(solution)/shard_map/all_gather | solution.py:44
  77.4 3.8 gather_fusion
  81.2 0.2 select_select_fusion.1
  81.5 6.3 while.10
  82.1 3.4 multiply_reduce_fusion.3
  85.5 1.5 dynamic_update_slice.5
  87.8 3.6 fusion.25
  91.4 8.1 copy.21
  99.5 0.0 reduce-scatter.2.cloned.1.call-update
  99.5 0.3 all-gather.8.cloned.1.call-start
  99.7 39.3 %all-reduce.3.cloned.1.call-done = (f32[128,128]{0,1:T(8,128)}, f32[128,128]{0,1:T(8,128)}) async-done(((f32[128,128]{0,1:T(8,128)}, f32[128,128]{0,1:T(8,128)}), (f32[128,128]{0,1:T(8,128)}, f32[128,128]{0,1:T(8,128)})) %all-reduce.3.cloned.1.call-update) | async-done | bytes 131088 | tf_op jit(solution)/shard_map/psum | solution.py:89
  139.1 0.9 mul.47
  140.0 0.1 copy.19
  140.1 11.7 %cholesky.16 = f32[128,128]{1,0:T(8,128)S(1)} custom-call(f32[128,128]{1,0:T(8,128)S(1)} %fusion.13), custom_call_target="Cholesky" | custom-call | tf_op jit(solution)/shard_map/jit(cholesky)/cholesky | solution.py:91
  151.8 0.6 compare_reduce_fusion
  152.5 0.7 fusion.8
  153.1 9.8 %custom-call.10 = f32[1,128,128]{1,2,0:T(8,128)S(1)} custom-call(f32[1,128,128]{2,1,0:T(8,128)S(1)} %fusion.8), custom_call_target="InvertDiagBlocksLowerTriangular" | custom-call | tf_op jit(solution)/shard_map/jit(_cho_solve)/triangular_solve | solution.py:92
  163.0 628.2 %reduce-scatter.2.cloned.1.call-done = f32[128,128]{1,0:T(8,128)} async-done(((f32[16384,128]{1,0:T(8,128)}), f32[128,128]{1,0:T(8,128)}) %reduce-scatter.2.cloned.1.call-update) | async-done | bytes 65552 | tf_op jit(solution)/shard_map/reduce_scatter | solution.py:83
  791.2 1.1 fusion.11
  792.3 0.9 fusion.9
  793.2 0.0 all-gather.8.cloned.1.call-update
  793.3 36.5 %all-gather.8.cloned.1.call-done = f32[2048,128]{1,0:T(8,128)} async-done(((f32[128,128]{1,0:T(8,128)}), f32[2048,128]{1,0:T(8,128)}) %all-gather.8.cloned.1.call-update) | async-done | bytes 1048592 | tf_op jit(solution)/shard_map/all_gather | solution.py:93
  829.7 2.3 copy.37
  (9 shorter events, 0.2 us)
Async XLA Ops:
  6.5 37.1 %all-gather.6.cloned.1.call-start = ((), (), s32[]{:S(2)}) async-start(), calls=%async_computation.2 | async-start | bytes 4718592 | tf_op jit(solution)/shard_map/all_gather | solution.py:43
  7.3 70.2 %all-gather.4.cloned.1.call-start = ((), (), s32[]{:S(2)}) async-start(), calls=%async_computation.1 | async-start | bytes 4718592 | tf_op jit(solution)/shard_map/all_gather | solution.py:44
  8.0 131.1 %all-reduce.3.cloned.1.call-start = ((), (), s32[]{:S(2)}) async-start(), calls=%async_computation.5 | async-start | bytes 262144 | tf_op jit(solution)/shard_map/psum | solution.py:89
  12.4 778.8 %reduce-scatter.2.cloned.1.call-start = ((), (), s32[]{:S(2)}) async-start(), calls=%async_computation.3 | async-start | bytes 8454144 | tf_op jit(solution)/shard_map/reduce_scatter | solution.py:83
  99.5 730.3 %all-gather.8.cloned.1.call-start = ((), (), s32[]{:S(2)}) async-start(), calls=%async_computation.4 | async-start | bytes 1114112 | tf_op jit(solution)/shard_map/all_gather | solution.py:93
Sparse Core Ops, SparseCore 0:
  9.1 34.5 all-gather.5
  45.4 32.0 all-gather.3
  79.8 59.2 all-reduce.2
  141.4 649.7 reduce-scatter.1
  793.4 36.3 all-gather.7
where the time goes:
time: 839 us
  waiting for transfers between devices  763 us (91%)
  other arithmetic  27.2 us (3%)
  local copies, waits for them, and re-layouts  19.7 us (2%)
  matrix products  13.4 us (2%)
  between operations  13.3 us (2%)
    reduce_scatter x1, waiting for transfers between devices, body(): lax.psum_scatter(summed.reshape(lax.axis_size(('tiles', 'rows')) * owned_...  628 us
    psum x1, waiting for transfers between devices, body(): lax.psum((factor_gram(factor_b), factor_gram(factor_c)), 'rows')  39.3 us
    all_gather x1, waiting for transfers between devices, body(): return lax.all_gather(solved, 'tiles', axis=0, tiled=True)  36.5 us
    all_gather x1, waiting for transfers between devices, body(): lax.all_gather(factor_c, 'rows', axis=0, tiled=True)  29.8 us
    all_gather x1, waiting for transfers between devices, body(): lax.all_gather(factor_b, 'rows', axis=0, tiled=True)  27.9 us
  transfers between devices with their start and end apart: 5, of which 5 were waited for; matrix products, arithmetic and copies ran while one was open for 7% of the time, Pallas kernels for 0%

commit v1 on v0

--- a/solution.py
+++ b/solution.py
@@ -2,6 +2,39 @@
 import jax.numpy as jnp
 from jax import lax
 from jax.sharding import PartitionSpec as P
+from jax.lax import axis_index, axis_size, ppermute
+
+
+def switch_blocks(array_in, array_axis):
+    x_next = list(array_in.shape[1:])
+    x_next[array_axis] *= array_in.shape[0]
+    step_out = jnp.moveaxis(array_in, 0, array_axis).reshape(x_next)
+    return step_out
+
+
+def clear_the_scales(bus_axis, on_dim, patch):
+    n_peers_all = axis_size(bus_axis)
+    samples = []
+    for q in range(n_peers_all):
+        samples.append((q, (q + 1) % n_peers_all))
+    blocks_here = []
+    for m, jj in samples:
+        blocks_here.append((jj, m))
+    w_next, item_now = ([], [])
+    for tick in range(n_peers_all - 1):
+        if tick % 2 == 0:
+            side_arr = ppermute(w_next[-1] if w_next else patch, bus_axis, samples)
+            w_next.append(side_arr)
+        else:
+            clean = ppermute(item_now[-1] if item_now else patch, bus_axis, blocks_here)
+            item_now.append(clean)
+    built = jnp.stack([*w_next[::-1], patch, *item_now])
+    response = axis_index(bus_axis)
+    known = len(w_next)
+    outer = response - known
+    built = built[(jnp.arange(n_peers_all) - outer) % n_peers_all]
+    block_last = switch_blocks(built, on_dim)
+    return block_last
 
 
 def slot_table(device, tile_coords, tile_owner, slot_count):
@@ -41,7 +74,7 @@
     carry = (blank, blank)
     pieces = (
         lax.all_gather(factor_b, "rows", axis=0, tiled=True),
-        lax.all_gather(factor_c, "rows", axis=0, tiled=True),
+        clear_the_scales("rows", 0, factor_c),
     )
     results = []
     for held, piece, needed in zip(carry, pieces, (need_b, need_c)):

time: 839 us -> 815 us (0.971)
  waiting for transfers between devices: 763 us -> 718 us
  local copies, waits for them, and re-layouts: 19.7 us -> 31.7 us
  starting transfers between devices: 0.38 us -> 9.25 us
    ppermute x0 -> x7, waiting for transfers between devices: none -> 35.8 us  [the longest x4 35.8 us: clear_the_scales(): side_arr = ppermute(w_next[-1] if w_next else patch, bus_axis, samples)]
    all_gather x1 -> x0, waiting for transfers between devices: 29.8 us -> none  [body(): lax.all_gather(factor_c, 'rows', axis=0, tiled=True)]
    all_gather x1, waiting for transfers between devices: 27.9 us -> 0.02 us  [body(): lax.all_gather(factor_b, 'rows', axis=0, tiled=True)]
    psum x1, waiting for transfers between devices: 39.3 us -> 13.4 us  [body(): lax.psum((factor_gram(factor_b), factor_gram(factor_c)), 'rows')]
    ppermute x0 -> x7, starting transfers between devices: none -> 8.91 us  [the longest x3 8.87 us: clear_the_scales(): clean = ppermute(item_now[-1] if item_now else patch, bus_axis, blocks_here)]
  transfers between devices with their start and end apart: 5 -> 11, of which waited for: 5 -> 6; matrix products, arithmetic and copies ran while one was open for 7% -> 8% of each run, Pallas kernels for 0% -> 0%
where the time goes in v1:
time: 815 us; the launch traced here: 814 us
  waiting for transfers between devices  718 us (88%)
  local copies, waits for them, and re-layouts  31.7 us (4%)
  other arithmetic  27.2 us (3%)
  matrix products  13.5 us (2%)
  between operations  13.3 us (2%)
  starting transfers between devices  9.25 us (1%)
    reduce_scatter x1, waiting for transfers between devices, body(): lax.psum_scatter(summed.reshape(lax.axis_size(('tiles', 'rows')) * owned_...  631 us
    all_gather x1, waiting for transfers between devices, body(): return lax.all_gather(solved, 'tiles', axis=0, tiled=True)  37.5 us
    ppermute x4, waiting for transfers between devices, clear_the_scales(): side_arr = ppermute(w_next[-1] if w_next else patch, bus_axis, samples)  35.8 us
  transfers between devices with their start and end apart: 11, of which 6 were waited for; matrix products, arithmetic and copies ran while one was open for 8% of the time, Pallas kernels for 0%

profile of v1, /device:TPU:0, one launch (start us, length us, event | category | flops | bytes accessed | tf_op | source)
XLA Modules:
  0.0 814.5 jit_solution(18086778962422345229)
XLA Ops:
  6.5 0.7 all-gather.3.cloned.1.call-update
  7.3 2.9 collective-permute-start.4
  10.3 2.2 fusion.38
  12.4 2.2 fusion.39
  14.7 0.7 fusion.33
  15.4 0.3 reduce-window.9
  15.7 0.1 slice.34
  15.8 0.1 slice_reduce_fusion
  16.0 0.1 fusion.16
  16.2 0.6 convert_reduce_fusion
  16.8 0.8 multiply_reduce_fusion.1
  17.8 14.2 %collective-permute-done.1 = bf16[2048,128]{1,0:T(8,128)(2,1)S(1)} collective-permute-done((bf16[2048,128]{1,0:T(8,128)(2,1)S(1)}, bf16[2048,128]{1,0:T(8,128)(2,1)S(1)}, u32[]{:S(2)}, u32[]{:S(2)}) %collective-permute-start.1) | collective-permute-done | bytes 524320 | tf_op jit(solution)/shard_map/ppermute | solution.py:26
  32.1 3.0 collective-permute-start.5
  35.1 14.9 %collective-permute-done.2 = bf16[2048,128]{1,0:T(8,128)(2,1)S(1)} collective-permute-done((bf16[2048,128]{1,0:T(8,128)(2,1)S(1)}, bf16[2048,128]{1,0:T(8,128)(2,1)S(1)}, u32[]{:S(2)}, u32[]{:S(2)}) %collective-permute-start.2) | collective-permute-done | bytes 524320 | tf_op jit(solution)/shard_map/ppermute | solution.py:26
  50.0 0.1 compare_and_fusion
  50.1 3.0 collective-permute-start.6
  53.1 6.7 collective-permute-done.3
  59.8 0.8 bitcast_dynamic-update-slice_fusion.7
  60.6 0.9 bitcast_dynamic-update-slice_fusion.6
  61.4 0.8 bitcast_dynamic-update-slice_fusion.5
  62.3 0.8 bitcast_dynamic-update-slice_fusion.4
  63.1 0.8 bitcast_dynamic-update-slice_fusion.3
  64.0 0.9 bitcast_dynamic-update-slice_fusion.2
  64.8 0.8 bitcast_dynamic-update-slice_fusion.1
  65.6 0.8 bitcast_dynamic-update-slice_fusion
  66.5 5.3 gather_fusion
  71.7 3.8 gather_fusion.1
  75.5 0.2 select_select_fusion.1
  75.8 3.8 gather_fusion.2
  79.6 0.2 select_select_fusion
  79.8 6.4 while.10
  80.5 3.5 multiply_reduce_fusion.3
  84.0 1.5 dynamic_update_slice.5
  86.3 3.6 fusion.25
  89.9 8.1 copy.21
  98.0 0.3 all-gather.5.cloned.1.call-start
  98.2 13.4 %all-reduce.3.cloned.1.call-done = (f32[128,128]{0,1:T(8,128)}, f32[128,128]{0,1:T(8,128)}) async-done(((f32[128,128]{0,1:T(8,128)}, f32[128,128]{0,1:T(8,128)}), (f32[128,128]{0,1:T(8,128)}, f32[128,128]{0,1:T(8,128)})) %all-reduce.3.cloned.1.call-update) | async-done | bytes 131088 | tf_op jit(solution)/shard_map/psum | solution.py:122
  111.6 0.9 mul.47
  112.5 0.1 copy.19
  112.6 11.7 %cholesky.16 = f32[128,128]{1,0:T(8,128)S(1)} custom-call(f32[128,128]{1,0:T(8,128)S(1)} %fusion.13), custom_call_target="Cholesky" | custom-call | tf_op jit(solution)/shard_map/jit(cholesky)/cholesky | solution.py:124
  124.3 0.6 compare_reduce_fusion
  125.0 0.7 fusion.8
  125.7 9.8 %custom-call.10 = f32[1,128,128]{1,2,0:T(8,128)S(1)} custom-call(f32[1,128,128]{2,1,0:T(8,128)S(1)} %fusion.8), custom_call_target="InvertDiagBlocksLowerTriangular" | custom-call | tf_op jit(solution)/shard_map/jit(_cho_solve)/triangular_solve | solution.py:125
  135.5 630.6 %reduce-scatter.2.cloned.1.call-done = f32[128,128]{1,0:T(8,128)} async-done(((f32[16384,128]{1,0:T(8,128)}), f32[128,128]{1,0:T(8,128)}) %reduce-scatter.2.cloned.1.call-update) | async-done | bytes 65552 | tf_op jit(solution)/shard_map/reduce_scatter | solution.py:116
  766.1 1.1 fusion.11
  767.2 0.9 fusion.9
  768.1 37.5 %all-gather.5.cloned.1.call-done = f32[2048,128]{1,0:T(8,128)} async-done(((f32[128,128]{1,0:T(8,128)}), f32[2048,128]{1,0:T(8,128)}) %all-gather.5.cloned.1.call-update) | async-done | bytes 1048592 | tf_op jit(solution)/shard_map/all_gather | solution.py:126
  805.7 2.3 copy.44
  (32 shorter events, 0.7 us)
Async XLA Ops:
  6.5 56.6 %copy-start = (bf16[2048,128]{1,0:T(8,128)(2,1)S(1)}, bf16[2048,128]{1,0:T(8,128)(2,1)}, u32[]{:S(2)}) copy-start(bf16[2048,128]{1,0:T(8,128)(2,1)} %param.13) | copy-start | bytes 1572868
  6.5 69.2 %all-gather.3.cloned.1.call-start = ((), (), s32[]{:S(2)}) async-start(), calls=%async_computation.1 | async-start | bytes 4718592 | tf_op jit(solution)/shard_map/all_gather | solution.py:76
  7.3 104.3 %all-reduce.3.cloned.1.call-start = ((), (), s32[]{:S(2)}) async-start(), calls=%async_computation.4 | async-start | bytes 262144 | tf_op jit(solution)/shard_map/psum | solution.py:122
  7.3 10.3 %collective-permute-start = (bf16[2048,128]{1,0:T(8,128)(2,1)}, bf16[2048,128]{1,0:T(8,128)(2,1)S(1)}, u32[]{:S(2)}, u32[]{:S(2)}) collective-permute-start(bf16[2048,128]{1,0:T(8,128)(2,1)} %param.13), channel_id=1, source_target_pairs={{0,1},{1,2},{2,3},{3,4},{4,5},{5,6},{6,7},{7,0},{8,9},{9,10},{10,1... | collective-permute-start | bytes 1572872 | tf_op jit(solution)/shard_map/ppermute | solution.py:26
  7.3 24.8 %collective-permute-start.4 = (bf16[2048,128]{1,0:T(8,128)(2,1)}, bf16[2048,128]{1,0:T(8,128)(2,1)S(1)}, u32[]{:S(2)}, u32[]{:S(2)}) collective-permute-start(bf16[2048,128]{1,0:T(8,128)(2,1)} %param.13), channel_id=1, source_target_pairs={{1,0},{2,1},{3,2},{4,3},{5,4},{6,5},{7,6},{0,7},{9,8},{10,9},{11,1... | collective-permute-start | bytes 1572872 | tf_op jit(solution)/shard_map/ppermute | solution.py:29
  14.7 751.4 %reduce-scatter.2.cloned.1.call-start = ((), (), s32[]{:S(2)}) async-start(), calls=%async_computation.2 | async-start | bytes 8454144 | tf_op jit(solution)/shard_map/reduce_scatter | solution.py:116
  17.6 14.4 %collective-permute-start.1 = (bf16[2048,128]{1,0:T(8,128)(2,1)S(1)}, bf16[2048,128]{1,0:T(8,128)(2,1)S(1)}, u32[]{:S(2)}, u32[]{:S(2)}) collective-permute-start(bf16[2048,128]{1,0:T(8,128)(2,1)S(1)} %collective-permute-done), channel_id=1, source_target_pairs={{0,1},{1,2},{2,3},{3,4},{4,5},{5,6},{6,7},{7,0},{8,9},{9,10},{10,1... | collective-permute-start | bytes 1572872 | tf_op jit(solution)/shard_map/ppermute | solution.py:26
  32.0 17.9 %collective-permute-start.2 = (bf16[2048,128]{1,0:T(8,128)(2,1)S(1)}, bf16[2048,128]{1,0:T(8,128)(2,1)S(1)}, u32[]{:S(2)}, u32[]{:S(2)}) collective-permute-start(bf16[2048,128]{1,0:T(8,128)(2,1)S(1)} %collective-permute-done.1), channel_id=1, source_target_pairs={{0,1},{1,2},{2,3},{3,4},{4,5},{5,6},{6,7},{7,0},{8,9},{9,10},{10,1... | collective-permute-start | bytes 1572872 | tf_op jit(solution)/shard_map/ppermute | solution.py:26
  32.1 18.0 %collective-permute-start.5 = (bf16[2048,128]{1,0:T(8,128)(2,1)S(1)}, bf16[2048,128]{1,0:T(8,128)(2,1)S(1)}, u32[]{:S(2)}, u32[]{:S(2)}) collective-permute-start(bf16[2048,128]{1,0:T(8,128)(2,1)S(1)} %collective-permute-done.4), channel_id=1, source_target_pairs={{1,0},{2,1},{3,2},{4,3},{5,4},{6,5},{7,6},{0,7},{9,8},{10,9},{11,1... | collective-permute-start | bytes 1572872 | tf_op jit(solution)/shard_map/ppermute | solution.py:29
  49.9 9.8 %collective-permute-start.3 = (bf16[2048,128]{1,0:T(8,128)(2,1)S(1)}, bf16[2048,128]{1,0:T(8,128)(2,1)S(1)}, u32[]{:S(2)}, u32[]{:S(2)}) collective-permute-start(bf16[2048,128]{1,0:T(8,128)(2,1)S(1)} %collective-permute-done.2), channel_id=1, source_target_pairs={{0,1},{1,2},{2,3},{3,4},{4,5},{5,6},{6,7},{7,0},{8,9},{9,10},{10,1... | collective-permute-start | bytes 1572872 | tf_op jit(solution)/shard_map/ppermute | solution.py:26
  50.1 15.5 %collective-permute-start.6 = (bf16[2048,128]{1,0:T(8,128)(2,1)S(1)}, bf16[2048,128]{1,0:T(8,128)(2,1)S(1)}, u32[]{:S(2)}, u32[]{:S(2)}) collective-permute-start(bf16[2048,128]{1,0:T(8,128)(2,1)S(1)} %collective-permute-done.5), channel_id=1, source_target_pairs={{1,0},{2,1},{3,2},{4,3},{5,4},{6,5},{7,6},{0,7},{9,8},{10,9},{11,1... | collective-permute-start | bytes 1572872 | tf_op jit(solution)/shard_map/ppermute | solution.py:29
  98.0 707.7 %all-gather.5.cloned.1.call-start = ((), (), s32[]{:S(2)}) async-start(), calls=%async_computation.3 | async-start | bytes 1114112 | tf_op jit(solution)/shard_map/all_gather | solution.py:126
Sparse Core Ops, SparseCore 0:
  9.1 40.9 all-gather.2
  52.4 59.1 all-reduce.2
  114.1 651.9 reduce-scatter.1
  768.2 37.3 all-gather.4
